TPU v7x, 32 devices: a whole 2x2x4 slice. The times are simulated.
32 devices in a mesh: groups: 2 (over x), expert: 16 (over z, y, core).
Axes of the slice: x: 2, y: 2, z: 4, core: 2. Of those that a mesh axis runs over, the one named last changes fastest.
Arguments:
- tokens: bfloat16 [2048, 2048], P(('groups', 'expert')), parts along dimension 0, may hold values from -6 to 6
- expert_ids: int32 [2048, 8], P(('groups', 'expert')), parts along dimension 0, may hold values from 0 to 15, as said below
- gate_weights: float32 [2048, 8], P(('groups', 'expert')), parts along dimension 0, may hold values from 0.05 to 0.5
- w_gate: bfloat16 [16, 2048, 768], P('expert'), may hold values from -0.125 to 0.125
- w_up: bfloat16 [16, 2048, 768], P('expert'), may hold values from -0.125 to 0.125
- w_down: bfloat16 [16, 768, 2048], P('expert'), may hold values from -0.21875 to 0.21875
Outputs:
- mixed: bfloat16 [2048, 2048], P(('groups', 'expert')), parts along dimension 0
There are 2 independent parts, one for each index of `groups`. A program takes and returns all parts, laid end to end along the dimension named above; an argument that names none is the same for every part. Nothing has to cross between parts.
Inputs may be any that keep to these rules, and one draw needn't show every extreme that they name: `expert_ids`: each token names 8 different experts. Exactly 2 experts are named exactly 64 times by the tokens of every device; every other expert is named at most 28 times by the tokens of one device, and in every draw some such expert is named exactly 28 times by the tokens of every device.
All inputs are finite; a program needn't handle non-finite values.
Results may differ from a plain program's by a relative error of at most 0.0057.
Values may be sent and summed in bfloat16 or wider, within the bound.
A program may use at most 128 MiB of HBM per device.

v0:
```python
import functools
import jax
import jax.numpy as jnp
from jax import lax
from jax.experimental import pallas as pl
from jax.experimental.pallas import tpu as pltpu
from jax.sharding import PartitionSpec as P

row_block = 256
pieces = 4
chunks = 4
hidden_tile = 256
vmem_budget = 48 * 2**20


def swiglu_rows(rows_in, weights):
    gate_part = jnp.dot(rows_in, weights[0], preferred_element_type=jnp.float32)
    up_part = jnp.dot(rows_in, weights[1], preferred_element_type=jnp.float32)
    hidden = (jax.nn.silu(gate_part) * up_part).astype(jnp.bfloat16)
    return jnp.dot(hidden, weights[2], preferred_element_type=jnp.float32).astype(jnp.bfloat16)


def run_blocks(source_rows, block_total, weights, results):

    def block_step(block_num, current):
        row_start = block_num * row_block
        rows_in = lax.dynamic_slice_in_dim(source_rows, row_start, row_block, 0)
        return lax.dynamic_update_slice_in_dim(current, swiglu_rows(rows_in, weights), row_start, 0)

    return lax.fori_loop(jnp.zeros((), jnp.int32), block_total, block_step, results)


def route_and_run(tokens, flat_ids, slot_rank, routed, capacity, device_count, own_weights):
    local_tokens, model_width = tokens.shape
    slot_total = flat_ids.shape[0]
    top_count = slot_total // local_tokens
    buffer_rows = device_count * capacity
    padded_rows = (buffer_rows + row_block - 1) // row_block * row_block
    send_slot = jnp.where(routed, flat_ids * capacity + slot_rank, buffer_rows)
    token_of_slot = jnp.arange(slot_total, dtype=jnp.int32) // top_count
    source_row = jnp.zeros((buffer_rows,), jnp.int32).at[send_slot].set(token_of_slot, mode="drop")
    slot_filled = jnp.zeros((buffer_rows,), jnp.int32).at[send_slot].set(1, mode="drop")
    send_counts = jnp.sum(slot_filled.reshape(device_count, capacity), axis=1)
    outgoing = jnp.where(slot_filled[:, None] > 0, tokens[source_row], jnp.zeros((), jnp.bfloat16))
    outgoing = outgoing.reshape(device_count, capacity, model_width)
    count_column = send_counts.astype(jnp.bfloat16).reshape(device_count, 1)
    incoming, arrived = (
        lax.all_to_all(outgoing, "expert", split_axis=0, concat_axis=0, tiled=True),
        lax.all_to_all(count_column, "expert", split_axis=0, concat_axis=0, tiled=True),
    )
    arrived_counts = arrived.reshape(-1).astype(jnp.int32)
    offsets = jnp.cumsum(arrived_counts) - arrived_counts
    live_total = jnp.sum(arrived_counts)
    slot_index = jnp.arange(buffer_rows, dtype=jnp.int32)
    source_of = slot_index // capacity
    within = slot_index % capacity
    is_live = within < arrived_counts[source_of]
    packed_pos = offsets[source_of] + within
    target_pos = jnp.where(is_live, packed_pos, padded_rows)
    compact_source = (
        jnp.full((padded_rows,), buffer_rows, jnp.int32).at[target_pos].set(slot_index, mode="drop")
    )
    flat_incoming = jnp.concatenate(
        [incoming.reshape(buffer_rows, model_width), jnp.zeros((1, model_width), jnp.bfloat16)],
        axis=0,
    )
    compact = flat_incoming[compact_source]
    block_need = (live_total + row_block - 1) // row_block
    results = run_blocks(
        compact, block_need, own_weights, jnp.zeros((padded_rows, model_width), jnp.bfloat16)
    )
    back_slots = results[jnp.where(is_live, packed_pos, 0)]
    back_slots = jnp.where(is_live[:, None], back_slots, jnp.zeros((), jnp.bfloat16))
    back_slots = back_slots.reshape(device_count, capacity, model_width)
    returned_rows = lax.all_to_all(back_slots, "expert", split_axis=0, concat_axis=0, tiled=True)
    picked = returned_rows.reshape(buffer_rows, model_width)[jnp.where(routed, send_slot, 0)]
    return jnp.where(routed[:, None], picked, jnp.zeros((), jnp.bfloat16))


def visit_order(depth, place):
    return sorted(range(depth), key=lambda g: (abs(g - place), g if 2 * place < depth else -g))


def fused_kernel(
    depth, x_hbm, t_hbm, wg_hbm, wu_hbm, wd_hbm, out_ref,
    rows, tiles, wg, wu, wd, hid, part, a_in, y_out, y_in, c_out, c_in, acc,
    w_sem, own_sem, sx, rx, st, rt, sa, ra, sy, ry, sc, rc,
):
    f32, bf16 = jnp.float32, jnp.bfloat16
    local, width = x_hbm.shape
    inner = wg.shape[1]
    me = lax.axis_index("expert")
    c = lax.rem(me, 2)
    y = lax.rem(me // 2, 2)
    z = me // 4
    own_slot = y * 2 + c
    group_of = []
    for step in range(depth):
        g = jnp.int32(0)
        for place in range(depth):
            g = g + jnp.where(z == place, visit_order(depth, place)[step], 0)
        group_of.append(g)
    sibling = {"expert": (z * 2 + y) * 2 + (1 - c)}
    across = {"expert": (z * 2 + (1 - y)) * 2 + c}

    def along(place):
        return {"expert": (place * 2 + y) * 2 + c}

    has_up, has_down = z < depth - 1, z > 0

    def signal(target):
        pl.semaphore_signal(barrier, inc=1, device_id=target, device_id_type=pl.DeviceIdType.MESH)

    barrier = pltpu.get_barrier_semaphore()
    signal(sibling)
    signal(across)
    pl.when(has_up)(lambda: signal(along(z + 1)))
    pl.when(has_down)(lambda: signal(along(z - 1)))
    pl.semaphore_wait(barrier, 2 + has_up.astype(jnp.int32) + has_down.astype(jnp.int32))

    def remote(src, dst, send, recv, target):
        return pltpu.make_async_remote_copy(
            src_ref=src, dst_ref=dst, send_sem=send, recv_sem=recv,
            device_id=target, device_id_type=pl.DeviceIdType.MESH,
        )

    pending = []

    def launch(copies, cond=None):
        def go():
            for copy in copies:
                copy.start()
        if cond is None:
            go()
        else:
            pl.when(cond)(go)
        pending.append((copies, cond))

    chunk_rows = local // chunks

    def chunk_copies(g, slot, h, src_x, src_t, at, target):
        part_rows = pl.ds(h * chunk_rows, chunk_rows)
        copies = [
            remote(
                src_x.at[part_rows], rows.at[g, slot, part_rows],
                sx.at[at, h], rx.at[g, slot, h], target,
            )
        ]
        if h == 0:
            copies.append(remote(src_t, tiles.at[g, slot], st.at[at], rt.at[g, slot], target))
        return copies

    def push(g, slot, h, at, target, cond=None):
        launch(chunk_copies(g, slot, h, rows.at[g, slot], tiles.at[g, slot], at, target), cond)

    def arrive(g, slot, h):
        for copy in chunk_copies(g, slot, h, rows.at[g, slot], tiles.at[g, slot], 0, sibling):
            copy.wait_recv()

    y_base, c_base = depth + 1, 2 * depth + 1
    for h in range(chunks):
        launch(chunk_copies(z, own_slot, h, x_hbm, t_hbm, 0, along(z + 1)), has_up)
        launch(chunk_copies(z, own_slot, h, x_hbm, t_hbm, 1, along(z - 1)), has_down)
        launch(chunk_copies(z, own_slot, h, x_hbm, t_hbm, y_base, across))
    for h in range(chunks):
        launch(chunk_copies(z, own_slot, h, x_hbm, t_hbm, c_base, sibling))
    own_copies = [
        pltpu.make_async_copy(x_hbm, rows.at[z, own_slot], own_sem.at[0]),
        pltpu.make_async_copy(t_hbm, tiles.at[z, own_slot], own_sem.at[1]),
    ]
    weight_copies = [
        pltpu.make_async_copy(wg_hbm.at[0], wg, w_sem.at[0]),
        pltpu.make_async_copy(wu_hbm.at[0], wu, w_sem.at[1]),
        pltpu.make_async_copy(wd_hbm.at[0], wd, w_sem.at[2]),
    ]
    for copy in own_copies + weight_copies:
        copy.start()

    def relay_chain(step, h):
        g = group_of[step]
        arrive(g, own_slot, h)
        onward = jnp.where(g < z, z + 1, z - 1)
        push(g, own_slot, h, 1 + step, along(onward), (onward >= 0) & (onward < depth))
        push(g, own_slot, h, y_base + step, across)
        push(g, own_slot, h, c_base + step, sibling)

    def relay_across(step, h):
        g = group_of[step]
        slot = (1 - y) * 2 + c
        arrive(g, slot, h)
        push(g, slot, h, c_base + depth + step, sibling)

    def await_sibling(step):
        g = group_of[step]
        for h in range(chunks):
            arrive(g, y * 2 + 1 - c, h)
            arrive(g, (1 - y) * 2 + 1 - c, h)

    def piece_of(p):
        return pl.ds(p * (width // pieces), width // pieces)

    def pair_copy(step, half, p):
        g = group_of[step]
        return remote(
            part.at[g, half * 2 + 1 - c, :, piece_of(p)], a_in.at[g, half, :, piece_of(p)],
            sa.at[step, half, p], ra.at[step, half, p], sibling,
        )

    def run_hidden(step, j):
        g = group_of[step]
        cols = pl.ds(j * hidden_tile, hidden_tile)
        block = rows[g].reshape(4 * local, width)
        gate = jnp.dot(block, wg[:, cols], preferred_element_type=f32)
        up = jnp.dot(block, wu[:, cols], preferred_element_type=f32)
        hid[:, cols] = (gate / (1.0 + jnp.exp(-gate)) * up).astype(bf16)

    def run_out(step):
        g = group_of[step]
        span = tiles.shape[3]
        lane = lax.broadcasted_iota(jnp.int32, (local, span), 1)
        line = lax.broadcasted_iota(jnp.int32, (local, span), 0)
        diagonal = (lane == line) | (lane == line + local)
        expert_row = lax.broadcasted_iota(jnp.int32, tiles.shape[2:], 0) == me
        scales = []
        for slot in range(4):
            mine = jnp.sum(
                jnp.where(expert_row, tiles[g, slot].astype(f32), 0.0), axis=0, keepdims=True
            )
            spread = jnp.broadcast_to(mine, (local, span))
            scales.append(jnp.sum(jnp.where(diagonal, spread, 0.0), axis=1, keepdims=True))
        for p in range(pieces):
            cols = piece_of(p)
            result = jnp.dot(hid[...], wd[:, cols], preferred_element_type=f32)
            for slot in range(4):
                scaled = result[slot * local : (slot + 1) * local] * scales[slot]
                part[g, slot, :, cols] = scaled.astype(bf16)
            for half in range(2):
                launch([pair_copy(step, half, p)])

    hidden_total = inner // hidden_tile

    def run_part(step, h):
        if h == 0:
            await_sibling(step)
            if step == 0:
                for copy in own_copies + weight_copies:
                    copy.wait()
        for j in range(hidden_total):
            if j * (chunks - 1) // hidden_total == h:
                run_hidden(step, j)
        if h == chunks - 1:
            run_out(step)

    def pair_sum(g, half, cols):
        return part[g, half * 2 + c, :, cols].astype(f32) + a_in[g, half, :, cols].astype(f32)

    def across_copy(step, p):
        return remote(
            y_out.at[step, :, piece_of(p)], y_in.at[step, :, piece_of(p)],
            sy.at[step, p], ry.at[step, p], across,
        )

    def send_across(step):
        g = group_of[step]
        for p in range(pieces):
            for half in range(2):
                pair_copy(step, half, p).wait_recv()
            y_out[step, :, piece_of(p)] = pair_sum(g, 1 - y, piece_of(p)).astype(bf16)
            launch([across_copy(step, p)])

    def chain_copy(step, way, g, p, target):
        return remote(
            c_out.at[step, :, piece_of(p)], c_in.at[way, g, :, piece_of(p)],
            sc.at[step, p], rc.at[way, g, p], target,
        )

    def add_chain(way, g, p):
        chain_copy(0, way, g, p, sibling).wait_recv()
        acc[...] += c_in[way, g, :, piece_of(p)].astype(f32)

    def send_chain(step):
        g = group_of[step]
        for p in range(pieces):
            cols = piece_of(p)
            across_copy(step, p).wait_recv()
            acc[...] = pair_sum(g, y, cols) + y_in[step, :, cols].astype(f32)
            if step == 0:
                pl.when(has_down)(lambda: add_chain(0, g, p))
                pl.when(has_up)(lambda: add_chain(1, g, p))
                out_ref[:, cols] = acc[...].astype(bf16)
            else:
                way = jnp.where(g > z, 0, 1)
                pl.when(((g > z) & has_down) | ((g < z) & has_up))(lambda: add_chain(way, g, p))
                c_out[step, :, cols] = acc[...].astype(bf16)
                launch([chain_copy(step, way, g, p, along(jnp.where(g > z, z + 1, z - 1)))])

    for turn in range(1, depth + 1):
        for h in range(chunks):
            if turn < depth:
                relay_chain(turn, h)
            relay_across(turn - 1, h)
            if turn >= 2:
                run_part(turn - 2, h)
    if depth > 2:
        send_across(depth - 2)
    for h in range(chunks):
        run_part(depth - 1, h)
    order = [depth - 2, depth - 1] + list(range(depth - 3, -1, -1))
    for step in order[1 if depth > 2 else 0 :]:
        send_across(step)
    for step in order:
        send_chain(step)
    for copies, cond in pending:
        def finish(copies=copies):
            for copy in copies:
                copy.wait_send()
        if cond is None:
            finish()
        else:
            pl.when(cond)(finish)


def fused_layer(tokens, tile, w_gate, w_up, w_down, depth):
    local, width = tokens.shape
    inner = w_gate.shape[2]
    bf16, f32 = jnp.bfloat16, jnp.float32
    dma = pltpu.SemaphoreType.DMA
    anywhere = pl.BlockSpec(memory_space=pl.ANY)
    sends = 4 * depth + 1
    return pl.pallas_call(
        functools.partial(fused_kernel, depth),
        out_shape=jax.ShapeDtypeStruct((local, width), bf16),
        in_specs=[anywhere] * 5,
        out_specs=pl.BlockSpec(memory_space=pltpu.VMEM),
        scratch_shapes=[
            pltpu.VMEM((depth, 4, local, width), bf16),
            pltpu.VMEM((depth, 4) + tile.shape, bf16),
            pltpu.VMEM((width, inner), bf16),
            pltpu.VMEM((width, inner), bf16),
            pltpu.VMEM((inner, width), bf16),
            pltpu.VMEM((4 * local, inner), bf16),
            pltpu.VMEM((depth, 4, local, width), bf16),
            pltpu.VMEM((depth, 2, local, width), bf16),
            pltpu.VMEM((depth, local, width), bf16),
            pltpu.VMEM((depth, local, width), bf16),
            pltpu.VMEM((depth, local, width), bf16),
            pltpu.VMEM((2, depth, local, width), bf16),
            pltpu.VMEM((local, width // pieces), f32),
            dma((3,)), dma((2,)),
            dma((sends, chunks)), dma((depth, 4, chunks)), dma((sends,)), dma((depth, 4)),
            dma((depth, 2, pieces)), dma((depth, 2, pieces)),
            dma((depth, pieces)), dma((depth, pieces)),
            dma((depth, pieces)), dma((2, depth, pieces)),
        ],
        compiler_params=pltpu.CompilerParams(
            collective_id=0, has_side_effects=True, vmem_limit_bytes=60 * 2**20
        ),
    )(tokens, tile, w_gate, w_up, w_down)


def choice_tile(expert_ids, gate_weights, expert_total):
    experts = jnp.arange(expert_total, dtype=jnp.int32)[:, None, None]
    chosen = experts == expert_ids[None, :, :]
    dense = jnp.sum(jnp.where(chosen, gate_weights[None, :, :], 0.0), axis=2)
    high = lax.reduce_precision(dense, 8, 7)
    return jnp.concatenate([high, dense - high], axis=1).astype(jnp.bfloat16)


def fits_fused(device_count, local_tokens, model_width, inner):
    gathered = 2 * device_count * local_tokens * model_width
    weights = 6 * model_width * inner
    return (
        device_count % 4 == 0
        and device_count >= 8
        and 2 * local_tokens % 128 == 0
        and local_tokens % (16 * chunks) == 0
        and model_width % (pieces * 128) == 0
        and inner % hidden_tile == 0
        and 4 * gathered + weights <= vmem_budget
    )


def shards(tokens, expert_ids, gate_weights, w_gate, w_up, w_down):
    device_count = lax.axis_size("expert")
    local_tokens, model_width = tokens.shape
    top_count = expert_ids.shape[1]
    expert_total = device_count * w_gate.shape[0]
    capacity = min(
        local_tokens, 4 * ((local_tokens * top_count + expert_total - 1) // expert_total)
    )
    if fits_fused(device_count, local_tokens, model_width, w_gate.shape[2]):
        tile = choice_tile(expert_ids, gate_weights, expert_total)
        return fused_layer(tokens, tile, w_gate, w_up, w_down, device_count // 4)
    flat_ids = expert_ids.reshape(-1)
    slot_total = flat_ids.shape[0]
    expert_range = jnp.arange(device_count, dtype=jnp.int32)
    onehot = (flat_ids[:, None] == expert_range[None, :]).astype(jnp.int32)
    slot_rank = jnp.sum(jnp.cumsum(onehot, axis=0) * onehot, axis=1) - 1
    own_weights = (w_gate[0], w_up[0], w_down[0])
    routed = jnp.ones((slot_total,), jnp.bool_)
    slot_values = route_and_run(
        tokens, flat_ids, slot_rank, routed, capacity, device_count, own_weights
    )
    picked = slot_values.reshape(local_tokens, top_count, model_width)
    mixed = jnp.sum(picked.astype(jnp.float32) * gate_weights[:, :, None], axis=1)
    return mixed.astype(jnp.bfloat16)


def solution(mesh):
    placed = (
        P(("groups", "expert"), None),
        P(("groups", "expert"), None),
        P(("groups", "expert"), None),
        P("expert", None, None),
        P("expert", None, None),
        P("expert", None, None),
    )
    return jax.shard_map(
        shards, mesh=mesh, in_specs=placed, out_specs=P(("groups", "expert"), None), check_vma=False
    )
```

profile of v0, /device:TPU:0, one launch (start us, length us, event | category | flops | bytes accessed | tf_op | source)
XLA Modules:
  0.0 65.7 jit_solution(15562176179813597583)
XLA Ops:
  0.0 0.7 %select_reduce_fusion = f32[16,64]{1,0:T(8,128)S(1)} fusion(f32[64,8]{0,1:T(8,128)} %param.8, s32[64,8]{0,1:T(8,128)} %param.7), kind=kLoop, calls=%fused_computation | loop fusion | flops 23552 | bytes 8192 | tf_op jit(solution)/shard_map/reduce_sum | solution.py:364
  0.7 0.7 %pad_maximum_fusion.t_hbm = bf16[16,128]{1,0:T(8,128)(2,1)} fusion(bf16[16,64]{1,0:T(8,128)(2,1)S(1)} %get-tuple-element.6, bf16[16,64]{1,0:T(8,128)(2,1)S(1)} %get-tuple-element.5), kind=kLoop, calls=%fused_computation.5 | loop fusion | flops 8192 | bytes 8192 | tf_op jit(solution)/shard_map/concatenate | solution.py:366
  1.4 62.6 %shard_map.64 = bf16[64,2048]{1,0:T(8,128)(2,1)} custom-call(bf16[64,2048]{1,0:T(8,128)(2,1)} %x_hbm.1, bf16[16,128]{1,0:T(8,128)(2,1)} %pad_maximum_fusion.t_hbm, bf16[1,2048,768]{2,1,0:T(8,128)(2,1)} %wg_hbm.1, bf16[1,2048,768]{2,1,0:T(8,128)(2,1)} %wu_hbm.1, bf16[1,768,2048]{2,1,0:T(8,128)(2,1)} %wd_hbm.1), custom_call_target="tpu_custom_call" | custom-call | tf_op jit(solution)/shard_map/pallas_call | solution.py:330
  64.0 1.7 %copy.10 = bf16[64,2048]{1,0:T(8,128)(2,1)} copy(bf16[64,2048]{1,0:T(8,128)(2,1)} %shard_map.64) | data formatting | bytes 524288
  (1 shorter events, 0.0 us)
where the time goes:
time: 65.9 us; the launch traced here: 65.7 us
  Pallas kernels  62.6 us (95%)
  local copies, waits for them, and re-layouts  1.67 us (3%)
  other arithmetic  1.4 us (2%)
    pallas_call x1, Pallas kernels, fused_layer(): pl.pallas_call(functools.partial(fused_kernel, depth), out_shape=jax.Shap...  62.6 us
    unnamed x1, local copies, waits for them, and re-layouts  1.67 us

commit v1 on v0

v1 whole, which is shorter than its diff:
```python
import functools
import jax
import jax.numpy as jnp
from jax import lax
from jax.experimental import pallas as pl
from jax.experimental.pallas import tpu as pltpu
from jax.sharding import PartitionSpec as P

row_block = 256
pieces = 8
chunks = 4
late_chunks = 1
z_pieces = 2
hidden_tile = 256
vmem_budget = 48 * 2**20


def swiglu_rows(rows_in, weights):
    gate_part = jnp.dot(rows_in, weights[0], preferred_element_type=jnp.float32)
    up_part = jnp.dot(rows_in, weights[1], preferred_element_type=jnp.float32)
    hidden = (jax.nn.silu(gate_part) * up_part).astype(jnp.bfloat16)
    return jnp.dot(hidden, weights[2], preferred_element_type=jnp.float32).astype(jnp.bfloat16)


def run_blocks(source_rows, block_total, weights, results):

    def block_step(block_num, current):
        row_start = block_num * row_block
        rows_in = lax.dynamic_slice_in_dim(source_rows, row_start, row_block, 0)
        return lax.dynamic_update_slice_in_dim(current, swiglu_rows(rows_in, weights), row_start, 0)

    return lax.fori_loop(jnp.zeros((), jnp.int32), block_total, block_step, results)


def route_and_run(tokens, flat_ids, slot_rank, routed, capacity, device_count, own_weights):
    local_tokens, model_width = tokens.shape
    slot_total = flat_ids.shape[0]
    top_count = slot_total // local_tokens
    buffer_rows = device_count * capacity
    padded_rows = (buffer_rows + row_block - 1) // row_block * row_block
    send_slot = jnp.where(routed, flat_ids * capacity + slot_rank, buffer_rows)
    token_of_slot = jnp.arange(slot_total, dtype=jnp.int32) // top_count
    source_row = jnp.zeros((buffer_rows,), jnp.int32).at[send_slot].set(token_of_slot, mode="drop")
    slot_filled = jnp.zeros((buffer_rows,), jnp.int32).at[send_slot].set(1, mode="drop")
    send_counts = jnp.sum(slot_filled.reshape(device_count, capacity), axis=1)
    outgoing = jnp.where(slot_filled[:, None] > 0, tokens[source_row], jnp.zeros((), jnp.bfloat16))
    outgoing = outgoing.reshape(device_count, capacity, model_width)
    count_column = send_counts.astype(jnp.bfloat16).reshape(device_count, 1)
    incoming, arrived = (
        lax.all_to_all(outgoing, "expert", split_axis=0, concat_axis=0, tiled=True),
        lax.all_to_all(count_column, "expert", split_axis=0, concat_axis=0, tiled=True),
    )
    arrived_counts = arrived.reshape(-1).astype(jnp.int32)
    offsets = jnp.cumsum(arrived_counts) - arrived_counts
    live_total = jnp.sum(arrived_counts)
    slot_index = jnp.arange(buffer_rows, dtype=jnp.int32)
    source_of = slot_index // capacity
    within = slot_index % capacity
    is_live = within < arrived_counts[source_of]
    packed_pos = offsets[source_of] + within
    target_pos = jnp.where(is_live, packed_pos, padded_rows)
    compact_source = (
        jnp.full((padded_rows,), buffer_rows, jnp.int32).at[target_pos].set(slot_index, mode="drop")
    )
    flat_incoming = jnp.concatenate(
        [incoming.reshape(buffer_rows, model_width), jnp.zeros((1, model_width), jnp.bfloat16)],
        axis=0,
    )
    compact = flat_incoming[compact_source]
    block_need = (live_total + row_block - 1) // row_block
    results = run_blocks(
        compact, block_need, own_weights, jnp.zeros((padded_rows, model_width), jnp.bfloat16)
    )
    back_slots = results[jnp.where(is_live, packed_pos, 0)]
    back_slots = jnp.where(is_live[:, None], back_slots, jnp.zeros((), jnp.bfloat16))
    back_slots = back_slots.reshape(device_count, capacity, model_width)
    returned_rows = lax.all_to_all(back_slots, "expert", split_axis=0, concat_axis=0, tiled=True)
    picked = returned_rows.reshape(buffer_rows, model_width)[jnp.where(routed, send_slot, 0)]
    return jnp.where(routed[:, None], picked, jnp.zeros((), jnp.bfloat16))


def visit_order(depth, place):
    return sorted(range(depth), key=lambda g: (abs(g - place), g if 2 * place < depth else -g))


def fused_kernel(
    depth, x_hbm, ids_ref, gates_ref, wg_hbm, wu_hbm, wd_hbm, out_ref,
    rows, tiles, wg, wu, wd, hid, part, a_in, y_out, y_in, c_out, c_in,
    w_sem, own_sem, sx, rx, st, rt, sa, ra, sy, ry, sc, rc,
):
    f32, bf16 = jnp.float32, jnp.bfloat16
    local, width = x_hbm.shape
    inner = wg.shape[1]
    span = width // pieces
    me = lax.axis_index("expert")
    c = lax.rem(me, 2)
    y = lax.rem(me // 2, 2)
    z = me // 4
    own_slot = y * 2 + c
    far_slot = (1 - y) * 2 + c
    group_of = []
    for step in range(depth):
        g = jnp.int32(0)
        for place in range(depth):
            g = g + jnp.where(z == place, visit_order(depth, place)[step], 0)
        group_of.append(g)
    sibling = {"expert": (z * 2 + y) * 2 + (1 - c)}
    across = {"expert": (z * 2 + (1 - y)) * 2 + c}

    def along(place):
        return {"expert": (place * 2 + y) * 2 + c}

    has_up, has_down = z < depth - 1, z > 0
    corner = (z == 0) | (z == depth - 1)

    own_copies = [pltpu.make_async_copy(x_hbm, rows.at[z, own_slot], own_sem.at[0])]
    weight_copies = [
        pltpu.make_async_copy(wg_hbm.at[0], wg, w_sem.at[0]),
        pltpu.make_async_copy(wu_hbm.at[0], wu, w_sem.at[1]),
        pltpu.make_async_copy(wd_hbm.at[0], wd, w_sem.at[2]),
    ]

    def signal(target):
        pl.semaphore_signal(barrier, inc=1, device_id=target, device_id_type=pl.DeviceIdType.MESH)

    barrier = pltpu.get_barrier_semaphore()
    signal(sibling)
    signal(across)
    pl.when(has_up)(lambda: signal(along(z + 1)))
    pl.when(has_down)(lambda: signal(along(z - 1)))

    expert_row = lax.broadcasted_iota(jnp.int32, (tiles.shape[2], local), 0)
    dense = jnp.zeros((tiles.shape[2], local), f32)
    for k in range(ids_ref.shape[0]):
        dense += jnp.where(ids_ref[k : k + 1, :] == expert_row, gates_ref[k : k + 1, :], 0.0)
    tiles[z, own_slot] = jnp.zeros(tiles.shape[2:], f32)
    tiles[z, own_slot, :, :local] = dense

    pl.semaphore_wait(barrier, 2 + has_up.astype(jnp.int32) + has_down.astype(jnp.int32))

    def remote(src, dst, send, recv, target):
        return pltpu.make_async_remote_copy(
            src_ref=src, dst_ref=dst, send_sem=send, recv_sem=recv,
            device_id=target, device_id_type=pl.DeviceIdType.MESH,
        )

    pending = []
    counts = {"x": 0, "t": 0}

    def launch(copies, cond=None):
        def go():
            for copy in copies:
                copy.start()
        if cond is None:
            go()
        else:
            pl.when(cond)(go)
        pending.append((copies, cond))

    chunk_rows = local // chunks
    early = list(range(chunks - late_chunks))
    late = list(range(chunks - late_chunks, chunks))

    def chunk_copy(g, slot, h, src, send, target):
        part_rows = pl.ds(h * chunk_rows, chunk_rows)
        return remote(src.at[part_rows], rows.at[g, slot, part_rows], send, rx.at[g, slot, h], target)

    def tile_copy(g, slot, send, target):
        return remote(tiles.at[g, slot], tiles.at[g, slot], send, rt.at[g, slot], target)

    def push(g, slot, h, target, cond=None, src=None):
        src = rows.at[g, slot] if src is None else src
        copies = [chunk_copy(g, slot, h, src, sx.at[counts["x"]], target)]
        counts["x"] += 1
        launch(copies, cond)

    def push_tile(g, slot, target, cond=None):
        copies = [tile_copy(g, slot, st.at[counts["t"]], target)]
        counts["t"] += 1
        launch(copies, cond)

    def arrive(g, slot, h):
        chunk_copy(g, slot, h, rows.at[g, slot], sx.at[0], sibling).wait_recv()
        if h == 0:
            tile_copy(g, slot, st.at[0], sibling).wait_recv()

    for h in range(chunks):
        push(z, own_slot, h, along(z + 1), has_up, src=x_hbm)
        push(z, own_slot, h, along(z - 1), has_down, src=x_hbm)
        push(z, own_slot, (late + early)[h], across, src=x_hbm)
        if h == 0:
            push_tile(z, own_slot, along(z + 1), has_up)
            push_tile(z, own_slot, along(z - 1), has_down)
            push_tile(z, own_slot, across)
    for h in range(chunks):
        push(z, own_slot, h, sibling, src=x_hbm)
    push_tile(z, own_slot, sibling)
    for copy in own_copies + weight_copies:
        copy.start()

    @pl.when(z == 0)
    def _():
        c_in[0] = jnp.zeros(c_in.shape[1:], bf16)

    @pl.when(z == depth - 1)
    def _():
        c_in[1] = jnp.zeros(c_in.shape[1:], bf16)

    def onward_of(g):
        onward = jnp.where(g < z, z + 1, z - 1)
        return along(onward), (onward >= 0) & (onward < depth)

    def relay_z(step, h):
        g = group_of[step]
        arrive(g, own_slot, h)
        target, cond = onward_of(g)
        push(g, own_slot, h, target, cond)
        if h in early:
            push(g, own_slot, h, across)
        if h == 0:
            push_tile(g, own_slot, target, cond)
            push_tile(g, own_slot, across)
        push(g, own_slot, h, sibling)
        if h == 0:
            push_tile(g, own_slot, sibling)

    def relay_far_z(step):
        g = group_of[step]
        for h in late:
            arrive(g, far_slot, h)
            target, cond = onward_of(g)
            push(g, far_slot, h, target, cond)
            push(g, far_slot, h, sibling)

    def relay_y(step, h):
        g = group_of[step]
        arrive(g, far_slot, h)
        if step == 0 and h in late:
            push(g, far_slot, h, along(z + 1), has_up)
            push(g, far_slot, h, along(z - 1), has_down)
        push(g, far_slot, h, sibling)
        if h == 0:
            push_tile(g, far_slot, sibling)

    def await_sibling(step, k):
        g = group_of[step]
        column = y if k == 0 else 1 - y
        for h in range(chunks):
            arrive(g, column * 2 + 1 - c, h)
        if step == 0 and k == 0:
            for copy in own_copies + weight_copies:
                copy.wait()

    def column_of(k):
        return y if k == 0 else 1 - y

    def run_hidden(step, k):
        await_sibling(step, k)
        g = group_of[step]
        for j in range(inner // hidden_tile):
            cols = pl.ds(j * hidden_tile, hidden_tile)
            block = rows[g, pl.ds(column_of(k) * 2, 2)].reshape(2 * local, width)
            gate = jnp.dot(block, wg[:, cols], preferred_element_type=f32)
            up = jnp.dot(block, wu[:, cols], preferred_element_type=f32)
            hid[:, cols] = (gate / (1.0 + jnp.exp(-gate)) * up).astype(bf16)

    ranges = [(0, z_pieces), (z_pieces, (pieces + z_pieces) // 2), ((pieces + z_pieces) // 2, pieces)]

    def pair_copy(step, k, r):
        lo, hi = ranges[r]
        some = pl.ds(lo, hi - lo)
        return remote(
            part.at[step, k, 1 - c, some], a_in.at[step, k, some],
            sa.at[step, k, r], ra.at[step, k, r], sibling,
        )

    def run_out(step, k):
        g = group_of[step]
        lanes = tiles.shape[3]
        lane = lax.broadcasted_iota(jnp.int32, (local, lanes), 1)
        line = lax.broadcasted_iota(jnp.int32, (local, lanes), 0)
        own_row = lax.broadcasted_iota(jnp.int32, tiles.shape[2:], 0) == me
        scales = []
        for core in range(2):
            mine = jnp.sum(
                jnp.where(own_row, tiles[g, column_of(k) * 2 + core], 0.0), axis=0, keepdims=True
            )
            spread = jnp.broadcast_to(mine, (local, lanes))
            scales.append(jnp.sum(jnp.where(lane == line, spread, 0.0), axis=1, keepdims=True))
        for r, (lo, hi) in enumerate(ranges):
            for p in range(lo, hi):
                result = jnp.dot(hid[...], wd[:, pl.ds(p * span, span)], preferred_element_type=f32)
                for core in range(2):
                    scaled = result[core * local : (core + 1) * local] * scales[core]
                    part[step, k, core, p] = scaled.astype(bf16)
            launch([pair_copy(step, k, r)])

    paired = set()

    def pair_sum(step, k, p):
        r = [lo <= p < hi for lo, hi in ranges].index(True)
        if (step, k, r) not in paired:
            paired.add((step, k, r))
            pair_copy(step, k, r).wait_recv()
        return part[step, k, c, p].astype(f32) + a_in[step, k, p].astype(f32)

    def await_pairs(step, k, lo, hi):
        for r, (first, last) in enumerate(ranges):
            if first < hi and last > lo and (step, k, r) not in paired:
                paired.add((step, k, r))
                pair_copy(step, k, r).wait_recv()

    def across_copy(step, p):
        return remote(
            y_out.at[step, p], y_in.at[step, p], sy.at[step, p], ry.at[step, p], across
        )

    def send_across(step):
        for p in range(z_pieces, pieces):
            y_out[step, p] = pair_sum(step, 1, p).astype(bf16)
            launch([across_copy(step, p)])

    def chain_copy(step, way, g, j, target):
        return remote(
            c_out.at[step, j], c_in.at[way, g, j], sc.at[step, j], rc.at[way, g, j], target
        )

    def hop(step, j, value, cond=None, first=False):
        g = group_of[step]
        way = jnp.where(g > z, 0, 1)
        copy = chain_copy(step, way, g, j, along(jnp.where(g > z, z + 1, z - 1)))

        def go():
            if first:
                c_out[step, j] = value().astype(bf16)
            else:
                pl.when(jnp.logical_not(corner))(
                    lambda: chain_copy(0, way, g, j, sibling).wait_recv()
                )
                c_out[step, j] = (value() + c_in[way, g, j].astype(f32)).astype(bf16)
            copy.start()

        if cond is None:
            go()
        else:
            pl.when(cond)(go)

    def note_hop(step, j):
        g = group_of[step]
        way = jnp.where(g > z, 0, 1)
        pending.append(
            ([chain_copy(step, way, g, j, along(jnp.where(g > z, z + 1, z - 1)))], None)
        )

    def chain_split(step, k, cond=None, first=False):
        await_pairs(step, k, 0, z_pieces)
        for q in range(z_pieces):
            j = q if k == 0 else pieces + q
            hop(step, j, lambda: pair_sum(step, k, q), cond, first)

    def chain_whole(step):
        for p in range(z_pieces, pieces):
            across_copy(step, p).wait_recv()
            hop(step, p, lambda: pair_sum(step, 0, p) + y_in[step, p].astype(f32))

    def await_ends(j):
        pl.when(has_down)(lambda: chain_copy(0, 0, z, j, sibling).wait_recv())
        pl.when(has_up)(lambda: chain_copy(0, 1, z, j, sibling).wait_recv())

    def ends(j):
        return c_in[0, z, j].astype(f32) + c_in[1, z, j].astype(f32)

    def early_chain(step):
        if 0 < step < depth:
            for k in range(2):
                chain_split(step, k, corner, True)

    last = depth - 1
    for h in late:
        relay_y(0, h)
    for t in range(1, depth):
        for h in range(chunks):
            relay_z(t, h)
            if h in early:
                relay_y(t - 1, h)
            if h == 0:
                run_hidden(t - 1, 0)
            if h == 1:
                run_out(t - 1, 0)
                if t > 1:
                    relay_far_z(t)
            if h == 2:
                if t >= 2:
                    early_chain(t - 2)
        if t == 1:
            relay_far_z(t)
        run_hidden(t - 1, 1)
        run_out(t - 1, 1)
    relay_y(last, 0)
    run_hidden(last, 0)
    early_chain(last - 1)
    for h in early[1:]:
        relay_y(last, h)
    run_out(last, 0)
    if depth > 2:
        send_across(last - 1)
    run_hidden(last, 1)
    run_out(last, 1)
    middle = jnp.logical_not(corner)
    order = ([last - 1] if depth > 2 else []) + [last] + list(range(last - 2, 0, -1))
    sends = order[1 if depth > 2 else 0 :] + [0]
    for at, step in enumerate(order):
        if at < len(sends):
            send_across(sends[at])
        for k in range(2):
            if step == last:
                chain_split(step, k)
            else:
                chain_split(step, k, middle)
        chain_whole(step)
    for step in sends[len(order) :]:
        send_across(step)
    for q in range(z_pieces):
        await_ends(pieces + q)
        y_out[0, q] = (pair_sum(0, 1, q) + ends(pieces + q)).astype(bf16)
        launch([across_copy(0, q)])
    for p in list(range(z_pieces, pieces)) + list(range(z_pieces)):
        await_ends(p)
        total = pair_sum(0, 0, p) + ends(p)
        across_copy(0, p).wait_recv()
        out_ref[:, pl.ds(p * span, span)] = (total + y_in[0, p].astype(f32)).astype(bf16)
    for step in range(1, depth):
        for j in range(pieces + z_pieces):
            note_hop(step, j)
    for copies, cond in pending:
        def finish(copies=copies):
            for copy in copies:
                copy.wait_send()
        if cond is None:
            finish()
        else:
            pl.when(cond)(finish)


def fused_layer(tokens, ids, gates, w_gate, w_up, w_down, expert_total, depth):
    local, width = tokens.shape
    inner = w_gate.shape[2]
    bf16, f32 = jnp.bfloat16, jnp.float32
    dma = pltpu.SemaphoreType.DMA
    anywhere = pl.BlockSpec(memory_space=pl.ANY)
    inside = pl.BlockSpec(memory_space=pltpu.VMEM)
    span = width // pieces
    sends = depth * (6 * chunks + 2)
    lots = pieces + z_pieces
    return pl.pallas_call(
        functools.partial(fused_kernel, depth),
        out_shape=jax.ShapeDtypeStruct((local, width), bf16),
        in_specs=[anywhere, inside, inside] + [anywhere] * 3,
        out_specs=pl.BlockSpec(memory_space=pltpu.VMEM),
        scratch_shapes=[
            pltpu.VMEM((depth, 4, local, width), bf16),
            pltpu.VMEM((depth, 4, expert_total, 128), f32),
            pltpu.VMEM((width, inner), bf16),
            pltpu.VMEM((width, inner), bf16),
            pltpu.VMEM((inner, width), bf16),
            pltpu.VMEM((2 * local, inner), bf16),
            pltpu.VMEM((depth, 2, 2, pieces, local, span), bf16),
            pltpu.VMEM((depth, 2, pieces, local, span), bf16),
            pltpu.VMEM((depth, pieces, local, span), bf16),
            pltpu.VMEM((depth, pieces, local, span), bf16),
            pltpu.VMEM((depth, lots, local, span), bf16),
            pltpu.VMEM((2, depth, lots, local, span), bf16),
            dma((3,)), dma((1,)),
            dma((sends,)), dma((depth, 4, chunks)), dma((5 * depth,)), dma((depth, 4)),
            dma((depth, 2, 3)), dma((depth, 2, 3)),
            dma((depth, pieces)), dma((depth, pieces)),
            dma((depth, lots)), dma((2, depth, lots)),
        ],
        compiler_params=pltpu.CompilerParams(
            collective_id=0, has_side_effects=True, vmem_limit_bytes=60 * 2**20
        ),
    )(tokens, ids, gates, w_gate, w_up, w_down)


def fits_fused(device_count, local_tokens, model_width, inner):
    gathered = 2 * device_count * local_tokens * model_width
    weights = 6 * model_width * inner
    return (
        device_count % 4 == 0
        and device_count >= 8
        and local_tokens in (64, 128)
        and local_tokens % (16 * chunks) == 0
        and model_width % (pieces * 128) == 0
        and inner % hidden_tile == 0
        and 4 * gathered + weights <= vmem_budget
    )


def shards(tokens, expert_ids, gate_weights, w_gate, w_up, w_down):
    device_count = lax.axis_size("expert")
    local_tokens, model_width = tokens.shape
    top_count = expert_ids.shape[1]
    expert_total = device_count * w_gate.shape[0]
    capacity = min(
        local_tokens, 4 * ((local_tokens * top_count + expert_total - 1) // expert_total)
    )
    if fits_fused(device_count, local_tokens, model_width, w_gate.shape[2]):
        return fused_layer(
            tokens, expert_ids.T, gate_weights.T, w_gate, w_up, w_down, expert_total, device_count // 4
        )
    flat_ids = expert_ids.reshape(-1)
    slot_total = flat_ids.shape[0]
    expert_range = jnp.arange(device_count, dtype=jnp.int32)
    onehot = (flat_ids[:, None] == expert_range[None, :]).astype(jnp.int32)
    slot_rank = jnp.sum(jnp.cumsum(onehot, axis=0) * onehot, axis=1) - 1
    own_weights = (w_gate[0], w_up[0], w_down[0])
    routed = jnp.ones((slot_total,), jnp.bool_)
    slot_values = route_and_run(
        tokens, flat_ids, slot_rank, routed, capacity, device_count, own_weights
    )
    picked = slot_values.reshape(local_tokens, top_count, model_width)
    mixed = jnp.sum(picked.astype(jnp.float32) * gate_weights[:, :, None], axis=1)
    return mixed.astype(jnp.bfloat16)


def solution(mesh):
    placed = (
        P(("groups", "expert"), None),
        P(("groups", "expert"), None),
        P(("groups", "expert"), None),
        P("expert", None, None),
        P("expert", None, None),
        P("expert", None, None),
    )
    return jax.shard_map(
        shards, mesh=mesh, in_specs=placed, out_specs=P(("groups", "expert"), None), check_vma=False
    )
```

time: 65.9 us -> 68.5 us (1.039)
  Pallas kernels: 62.6 us -> 66.6 us
  other arithmetic: 1.4 us -> 0 us
    pallas_call x1, Pallas kernels: 62.6 us -> 66.6 us  [fused_layer(): pl.pallas_call(functools.partial(fused_kernel, depth), out_shape=jax.Shap...]
    reduce_sum x1 -> x0, other arithmetic: 0.73 us -> none  [choice_tile(): dense = jnp.sum(jnp.where(chosen, gate_weights[None, :, :], 0.0), axis=2)]
where the time goes in v1:
time: 68.5 us; the launch traced here: 68.3 us
  Pallas kernels  66.6 us (97%)
  local copies, waits for them, and re-layouts  1.67 us (2%)
    pallas_call x1, Pallas kernels, fused_layer(): pl.pallas_call(functools.partial(fused_kernel, depth), out_shape=jax.Shap...  66.6 us
    unnamed x1, local copies, waits for them, and re-layouts  1.67 us

profile of v1, /device:TPU:0, one launch (start us, length us, event | category | flops | bytes accessed | tf_op | source)
XLA Modules:
  0.0 68.3 jit_solution(4187709794481887027)
XLA Ops:
  0.0 66.6 %shard_map.64 = bf16[64,2048]{1,0:T(8,128)(2,1)} custom-call(bf16[64,2048]{1,0:T(8,128)(2,1)} %x_hbm.1, s32[8,64]{1,0:T(8,128)} %bitcast.2, f32[8,64]{1,0:T(8,128)} %bitcast.3, bf16[1,2048,768]{2,1,0:T(8,128)(2,1)} %wg_hbm.1, bf16[1,2048,768]{2,1,0:T(8,128)(2,1)} %wu_hbm.1, bf16[1,768,2048]{2,1,0:T(8,128)(2,1)} %wd_hbm.1), custom_call_target="tpu_custom_call" | custom-call | tf_op jit(solution)/shard_map/pallas_call | solution.py:455
  66.6 1.7 %copy.8 = bf16[64,2048]{1,0:T(8,128)(2,1)} copy(bf16[64,2048]{1,0:T(8,128)(2,1)} %shard_map.64) | data formatting | bytes 524288

commit v2 on v1

--- a/solution.py
+++ b/solution.py
@@ -7,10 +7,10 @@
 from jax.sharding import PartitionSpec as P
 
 row_block = 256
-pieces = 8
+pieces = 4
 chunks = 4
 late_chunks = 1
-z_pieces = 2
+z_pieces = 0
 hidden_tile = 256
 vmem_budget = 48 * 2**20
 
@@ -129,12 +129,12 @@
     pl.when(has_up)(lambda: signal(along(z + 1)))
     pl.when(has_down)(lambda: signal(along(z - 1)))
 
-    expert_row = lax.broadcasted_iota(jnp.int32, (tiles.shape[2], local), 0)
-    dense = jnp.zeros((tiles.shape[2], local), f32)
+    expert_row = lax.broadcasted_iota(jnp.int32, (tiles.shape[3], local), 0)
+    dense = jnp.zeros((tiles.shape[3], local), f32)
     for k in range(ids_ref.shape[0]):
         dense += jnp.where(ids_ref[k : k + 1, :] == expert_row, gates_ref[k : k + 1, :], 0.0)
-    tiles[z, own_slot] = jnp.zeros(tiles.shape[2:], f32)
-    tiles[z, own_slot, :, :local] = dense
+    tiles[z, c, y] = jnp.zeros(tiles.shape[3:], f32)
+    tiles[z, c, y, :, :local] = dense
 
     pl.semaphore_wait(barrier, 2 + has_up.astype(jnp.int32) + has_down.astype(jnp.int32))
 
@@ -144,109 +144,146 @@
             device_id=target, device_id_type=pl.DeviceIdType.MESH,
         )
 
-    pending = []
-    counts = {"x": 0, "t": 0}
-
-    def launch(copies, cond=None):
-        def go():
-            for copy in copies:
-                copy.start()
-        if cond is None:
-            go()
-        else:
-            pl.when(cond)(go)
-        pending.append((copies, cond))
-
     chunk_rows = local // chunks
     early = list(range(chunks - late_chunks))
     late = list(range(chunks - late_chunks, chunks))
-
-    def chunk_copy(g, slot, h, src, send, target):
-        part_rows = pl.ds(h * chunk_rows, chunk_rows)
-        return remote(src.at[part_rows], rows.at[g, slot, part_rows], send, rx.at[g, slot, h], target)
-
-    def tile_copy(g, slot, send, target):
-        return remote(tiles.at[g, slot], tiles.at[g, slot], send, rt.at[g, slot], target)
-
-    def push(g, slot, h, target, cond=None, src=None):
-        src = rows.at[g, slot] if src is None else src
-        copies = [chunk_copy(g, slot, h, src, sx.at[counts["x"]], target)]
-        counts["x"] += 1
-        launch(copies, cond)
-
-    def push_tile(g, slot, target, cond=None):
-        copies = [tile_copy(g, slot, st.at[counts["t"]], target)]
-        counts["t"] += 1
-        launch(copies, cond)
-
-    def arrive(g, slot, h):
-        chunk_copy(g, slot, h, rows.at[g, slot], sx.at[0], sibling).wait_recv()
-        if h == 0:
-            tile_copy(g, slot, st.at[0], sibling).wait_recv()
-
+    split = len(early) * chunk_rows
+    both = [(0, split), (split, local)]
+    places = {}
+
+    def place(name):
+        return sx.at[places.setdefault(name, len(places))]
+
+    def block(g, slot, lo, hi, name, recv, target, src=None):
+        some = pl.ds(lo, hi - lo)
+        source = rows.at[g, slot] if src is None else src
+        return remote(source.at[some], rows.at[g, slot, some], place(name), recv, target)
+
+    def chunk(g, slot, h, name, target, src=None, recv=None):
+        recv = rx.at[g, slot, h] if recv is None else recv
+        return block(g, slot, h * chunk_rows, (h + 1) * chunk_rows, name, recv, target, src)
+
+    def across_chunk(g, slot, h, name, src=None):
+        return chunk(g, slot, h, name, across, src, rx.at[g, slot, 0 if h in early else h])
+
+    def whole(g, slot, name, target, src=None):
+        return block(g, slot, 0, local, name, rx.at[g, slot, 0], target, src)
+
+    def tile_column():
+        return remote(tiles.at[z, c], tiles.at[z, c], st.at[1], rt.at[0], sibling)
+
+    def tile_layer(g, send, target):
+        return remote(tiles.at[g], tiles.at[g], st.at[send], rt.at[2 + g], target)
+
+    own_tile = remote(tiles.at[z, c, y], tiles.at[z, c, y], st.at[0], rt.at[1], across)
+    own_tile.start()
     for h in range(chunks):
-        push(z, own_slot, h, along(z + 1), has_up, src=x_hbm)
-        push(z, own_slot, h, along(z - 1), has_down, src=x_hbm)
-        push(z, own_slot, (late + early)[h], across, src=x_hbm)
-        if h == 0:
-            push_tile(z, own_slot, along(z + 1), has_up)
-            push_tile(z, own_slot, along(z - 1), has_down)
-            push_tile(z, own_slot, across)
-    for h in range(chunks):
-        push(z, own_slot, h, sibling, src=x_hbm)
-    push_tile(z, own_slot, sibling)
+        pl.when(has_up)(lambda: chunk(z, own_slot, h, "up", along(z + 1), x_hbm).start())
+        pl.when(has_down)(lambda: chunk(z, own_slot, h, "down", along(z - 1), x_hbm).start())
+        across_chunk(z, own_slot, (late + early)[h], "across", x_hbm).start()
+    whole(z, own_slot, "sibling", sibling, x_hbm).start()
     for copy in own_copies + weight_copies:
         copy.start()
 
     @pl.when(z == 0)
     def _():
-        c_in[0] = jnp.zeros(c_in.shape[1:], bf16)
+        c_in[0, 0] = jnp.zeros(c_in.shape[2:], bf16)
 
     @pl.when(z == depth - 1)
     def _():
-        c_in[1] = jnp.zeros(c_in.shape[1:], bf16)
-
-    def onward_of(g):
-        onward = jnp.where(g < z, z + 1, z - 1)
-        return along(onward), (onward >= 0) & (onward < depth)
-
-    def relay_z(step, h):
-        g = group_of[step]
-        arrive(g, own_slot, h)
-        target, cond = onward_of(g)
-        push(g, own_slot, h, target, cond)
-        if h in early:
-            push(g, own_slot, h, across)
-        if h == 0:
-            push_tile(g, own_slot, target, cond)
-            push_tile(g, own_slot, across)
-        push(g, own_slot, h, sibling)
-        if h == 0:
-            push_tile(g, own_slot, sibling)
-
-    def relay_far_z(step):
-        g = group_of[step]
+        c_in[1, z] = jnp.zeros(c_in.shape[2:], bf16)
+
+    def share_tiles():
+        own_tile.wait_recv()
+        tile_column().start()
+        tile_column().wait_recv()
+        pl.when(has_up)(lambda: tile_layer(z, 2, along(z + 1)).start())
+        pl.when(has_down)(lambda: tile_layer(z, 3, along(z - 1)).start())
+
+    def ways_of(d):
+        return [
+            (0, z + d, z + d < depth, along(z - 1), has_down),
+            (1, z - d, z - d >= 0, along(z + 1), has_up),
+        ]
+
+    def relay_z(d, h):
+        for way, g, exists, onward, more in ways_of(d):
+            @pl.when(exists)
+            def _(way=way, g=g, onward=onward, more=more):
+                chunk(g, own_slot, h, "sibling", sibling).wait_recv()
+                pl.when(more)(lambda: chunk(g, own_slot, h, (d, way, 0), onward).start())
+                if h in early:
+                    across_chunk(g, own_slot, h, (d, way, 1)).start()
+                if h == chunks - 1:
+                    whole(g, own_slot, (d, way, 2), sibling).start()
+                    tile_layer(g, 0, sibling).wait_recv()
+                    pl.when(more)(lambda: tile_layer(g, 2 + 2 * d + way, onward).start())
+
+    def relay_far_z(d):
+        for way, g, exists, onward, more in ways_of(d):
+            @pl.when(exists)
+            def _(way=way, g=g, onward=onward, more=more):
+                for h in late:
+                    chunk(g, far_slot, h, "sibling", sibling).wait_recv()
+                    pl.when(more)(lambda: chunk(g, far_slot, h, (d, way, 3), onward).start())
+
+    def relay_far_y(d):
+        for way, g, exists, _, _ in ways_of(d):
+            @pl.when(exists)
+            def _(way=way, g=g):
+                block(g, far_slot, 0, split, "sibling", rx.at[g, far_slot, 0], sibling).wait_recv()
+                whole(g, far_slot, (d, way, 4), sibling).start()
+
+    def relay_late():
         for h in late:
-            arrive(g, far_slot, h)
-            target, cond = onward_of(g)
-            push(g, far_slot, h, target, cond)
-            push(g, far_slot, h, sibling)
-
-    def relay_y(step, h):
-        g = group_of[step]
-        arrive(g, far_slot, h)
-        if step == 0 and h in late:
-            push(g, far_slot, h, along(z + 1), has_up)
-            push(g, far_slot, h, along(z - 1), has_down)
-        push(g, far_slot, h, sibling)
-        if h == 0:
-            push_tile(g, far_slot, sibling)
+            chunk(z, far_slot, h, "sibling", sibling).wait_recv()
+            pl.when(has_up)(lambda: chunk(z, far_slot, h, "far_up", along(z + 1)).start())
+            pl.when(has_down)(lambda: chunk(z, far_slot, h, "far_down", along(z - 1)).start())
+
+    def relay_own_y():
+        block(z, far_slot, 0, split, "sibling", rx.at[z, far_slot, 0], sibling).wait_recv()
+        whole(z, far_slot, "far_sibling", sibling).start()
+
+    def sent(g, slot, lo, hi, name):
+        if hi > lo:
+            block(g, slot, lo, hi, name, rx.at[g, slot, 0], sibling).wait_send()
+
+    def finish_gather():
+        own_tile.wait_send()
+        tile_column().wait_send()
+        sent(z, own_slot, 0, local, "across")
+        sent(z, own_slot, 0, local, "sibling")
+        sent(z, far_slot, 0, local, "far_sibling")
+
+        @pl.when(has_up)
+        def _():
+            sent(z, own_slot, 0, local, "up")
+            sent(z, far_slot, split, local, "far_up")
+            tile_layer(z, 2, sibling).wait_send()
+
+        @pl.when(has_down)
+        def _():
+            sent(z, own_slot, 0, local, "down")
+            sent(z, far_slot, split, local, "far_down")
+            tile_layer(z, 3, sibling).wait_send()
+
+        for d in range(1, depth):
+            for way, g, exists, _, more in ways_of(d):
+                @pl.when(exists)
+                def _(way=way, g=g, more=more):
+                    sent(g, own_slot, 0, split, (d, way, 1))
+                    sent(g, own_slot, 0, local, (d, way, 2))
+                    sent(g, far_slot, 0, local, (d, way, 4))
+
+                    @pl.when(more)
+                    def _():
+                        sent(g, own_slot, 0, local, (d, way, 0))
+                        sent(g, far_slot, split, local, (d, way, 3))
+                        tile_layer(g, 2 + 2 * d + way, sibling).wait_send()
 
     def await_sibling(step, k):
         g = group_of[step]
-        column = y if k == 0 else 1 - y
-        for h in range(chunks):
-            arrive(g, column * 2 + 1 - c, h)
+        whole(g, column_of(k) * 2 + 1 - c, "sibling", sibling).wait_recv()
         if step == 0 and k == 0:
             for copy in own_copies + weight_copies:
                 copy.wait()
@@ -254,36 +291,42 @@
     def column_of(k):
         return y if k == 0 else 1 - y
 
-    def run_hidden(step, k):
-        await_sibling(step, k)
+    def run_hidden(step, k, j):
+        if j == 0:
+            await_sibling(step, k)
         g = group_of[step]
-        for j in range(inner // hidden_tile):
-            cols = pl.ds(j * hidden_tile, hidden_tile)
-            block = rows[g, pl.ds(column_of(k) * 2, 2)].reshape(2 * local, width)
-            gate = jnp.dot(block, wg[:, cols], preferred_element_type=f32)
-            up = jnp.dot(block, wu[:, cols], preferred_element_type=f32)
-            hid[:, cols] = (gate / (1.0 + jnp.exp(-gate)) * up).astype(bf16)
-
-    ranges = [(0, z_pieces), (z_pieces, (pieces + z_pieces) // 2), ((pieces + z_pieces) // 2, pieces)]
+        cols = pl.ds(j * hidden_tile, hidden_tile)
+        lines = rows[g, pl.ds(column_of(k) * 2, 2)].reshape(2 * local, width)
+        gate = jnp.dot(lines, wg[:, cols], preferred_element_type=f32)
+        up = jnp.dot(lines, wu[:, cols], preferred_element_type=f32)
+        hid[:, cols] = (gate / (1.0 + jnp.exp(-gate)) * up).astype(bf16)
+
+    def units(step, k):
+        tiles_of = [
+            functools.partial(run_hidden, step, k, j) for j in range(inner // hidden_tile)
+        ]
+        return tiles_of + [functools.partial(run_out, step, k)]
+
+    ranges = [(0, pieces // 2), (pieces // 2, pieces)]
 
     def pair_copy(step, k, r):
         lo, hi = ranges[r]
         some = pl.ds(lo, hi - lo)
         return remote(
             part.at[step, k, 1 - c, some], a_in.at[step, k, some],
-            sa.at[step, k, r], ra.at[step, k, r], sibling,
+            sa.at[step, k], ra.at[step, k, r], sibling,
         )
 
     def run_out(step, k):
         g = group_of[step]
-        lanes = tiles.shape[3]
+        lanes = tiles.shape[4]
         lane = lax.broadcasted_iota(jnp.int32, (local, lanes), 1)
         line = lax.broadcasted_iota(jnp.int32, (local, lanes), 0)
-        own_row = lax.broadcasted_iota(jnp.int32, tiles.shape[2:], 0) == me
+        own_row = lax.broadcasted_iota(jnp.int32, tiles.shape[3:], 0) == me
         scales = []
         for core in range(2):
             mine = jnp.sum(
-                jnp.where(own_row, tiles[g, column_of(k) * 2 + core], 0.0), axis=0, keepdims=True
+                jnp.where(own_row, tiles[g, core, column_of(k)], 0.0), axis=0, keepdims=True
             )
             spread = jnp.broadcast_to(mine, (local, lanes))
             scales.append(jnp.sum(jnp.where(lane == line, spread, 0.0), axis=1, keepdims=True))
@@ -293,7 +336,7 @@
                 for core in range(2):
                     scaled = result[core * local : (core + 1) * local] * scales[core]
                     part[step, k, core, p] = scaled.astype(bf16)
-            launch([pair_copy(step, k, r)])
+            pair_copy(step, k, r).start()
 
     paired = set()
 
@@ -312,56 +355,52 @@
 
     def across_copy(step, p):
         return remote(
-            y_out.at[step, p], y_in.at[step, p], sy.at[step, p], ry.at[step, p], across
+            y_out.at[step, p], y_in.at[step, p], sy.at[step], ry.at[step, p], across
         )
 
     def send_across(step):
         for p in range(z_pieces, pieces):
             y_out[step, p] = pair_sum(step, 1, p).astype(bf16)
-            launch([across_copy(step, p)])
+            across_copy(step, p).start()
 
     def chain_copy(step, way, g, j, target):
         return remote(
-            c_out.at[step, j], c_in.at[way, g, j], sc.at[step, j], rc.at[way, g, j], target
+            c_out.at[step, j], c_in.at[way, g, j], sc.at[step], rc.at[way, g, j], target
         )
 
-    def hop(step, j, value, cond=None, first=False):
+    last = depth - 1
+    middle = jnp.logical_not(corner)
+
+    def hop(step, j, value, relay):
         g = group_of[step]
         way = jnp.where(g > z, 0, 1)
-        copy = chain_copy(step, way, g, j, along(jnp.where(g > z, z + 1, z - 1)))
+        place_to = jnp.where(g > z, z + 1, z - 1)
+        if relay:
+            chain_copy(0, way, g, j, sibling).wait_recv()
+            value = value + c_in[way, g, j].astype(f32)
+        c_out[step, j] = value.astype(bf16)
+        chain_copy(step, way, g, j, along(place_to)).start()
+
+    def chain_split(step, cond=None, relay=False):
+        for k in range(2):
+            await_pairs(step, k, 0, z_pieces)
 
         def go():
-            if first:
-                c_out[step, j] = value().astype(bf16)
-            else:
-                pl.when(jnp.logical_not(corner))(
-                    lambda: chain_copy(0, way, g, j, sibling).wait_recv()
-                )
-                c_out[step, j] = (value() + c_in[way, g, j].astype(f32)).astype(bf16)
-            copy.start()
-
-        if cond is None:
-            go()
-        else:
-            pl.when(cond)(go)
-
-    def note_hop(step, j):
-        g = group_of[step]
-        way = jnp.where(g > z, 0, 1)
-        pending.append(
-            ([chain_copy(step, way, g, j, along(jnp.where(g > z, z + 1, z - 1)))], None)
-        )
-
-    def chain_split(step, k, cond=None, first=False):
-        await_pairs(step, k, 0, z_pieces)
-        for q in range(z_pieces):
-            j = q if k == 0 else pieces + q
-            hop(step, j, lambda: pair_sum(step, k, q), cond, first)
-
-    def chain_whole(step):
-        for p in range(z_pieces, pieces):
-            across_copy(step, p).wait_recv()
-            hop(step, p, lambda: pair_sum(step, 0, p) + y_in[step, p].astype(f32))
+            for k in range(2):
+                for q in range(z_pieces):
+                    hop(step, q if k == 0 else pieces + q, pair_sum(step, k, q), relay)
+
+        go() if cond is None else pl.when(cond)(go)
+
+    def chain_whole(step, cond=None, relay=False):
+        await_pairs(step, 0, z_pieces, pieces)
+
+        def go():
+            for p in range(z_pieces, pieces):
+                across_copy(step, p).wait_recv()
+                hop(step, p, pair_sum(step, 0, p) + y_in[step, p].astype(f32), relay)
+
+        go() if cond is None else pl.when(cond)(go)
 
     def await_ends(j):
         pl.when(has_down)(lambda: chain_copy(0, 0, z, j, sibling).wait_recv())
@@ -370,76 +409,77 @@
     def ends(j):
         return c_in[0, z, j].astype(f32) + c_in[1, z, j].astype(f32)
 
-    def early_chain(step):
-        if 0 < step < depth:
-            for k in range(2):
-                chain_split(step, k, corner, True)
-
-    last = depth - 1
-    for h in late:
-        relay_y(0, h)
-    for t in range(1, depth):
+    work = []
+
+    def drain(amount):
+        for _ in range(min(amount, len(work))):
+            work.pop(0)()
+
+    share_tiles()
+    relay_late()
+    for h in range(chunks):
+        relay_z(1, h)
+    relay_own_y()
+    work.extend(units(0, 0))
+    relay_far_z(1)
+    work.extend(units(0, 1))
+    for t in range(2, depth):
+        drain(2)
         for h in range(chunks):
             relay_z(t, h)
-            if h in early:
-                relay_y(t - 1, h)
-            if h == 0:
-                run_hidden(t - 1, 0)
+            drain(2)
             if h == 1:
-                run_out(t - 1, 0)
-                if t > 1:
-                    relay_far_z(t)
+                relay_far_y(t - 1)
+                work.extend(units(t - 1, 0) + units(t - 1, 1))
             if h == 2:
-                if t >= 2:
-                    early_chain(t - 2)
-        if t == 1:
-            relay_far_z(t)
-        run_hidden(t - 1, 1)
-        run_out(t - 1, 1)
-    relay_y(last, 0)
-    run_hidden(last, 0)
-    early_chain(last - 1)
-    for h in early[1:]:
-        relay_y(last, h)
-    run_out(last, 0)
-    if depth > 2:
-        send_across(last - 1)
-    run_hidden(last, 1)
-    run_out(last, 1)
-    middle = jnp.logical_not(corner)
-    order = ([last - 1] if depth > 2 else []) + [last] + list(range(last - 2, 0, -1))
-    sends = order[1 if depth > 2 else 0 :] + [0]
-    for at, step in enumerate(order):
-        if at < len(sends):
-            send_across(sends[at])
-        for k in range(2):
-            if step == last:
-                chain_split(step, k)
-            else:
-                chain_split(step, k, middle)
-        chain_whole(step)
-    for step in sends[len(order) :]:
-        send_across(step)
+                relay_far_z(t)
+        if t == 2:
+            pass
+        else:
+            work.append(functools.partial(chain_split, t - 2, corner))
+    drain(len(work))
+    relay_far_y(last)
+    work.extend(units(last, 0))
+    work.append(functools.partial(chain_split, last - 1, corner))
+    work.append(functools.partial(send_across, last - 1))
+    work.extend(units(last, 1))
+    drain(len(work))
+    send_across(last)
+    send_across(last - 2)
+    send_across(0)
+    chain_split(last, corner)
+    chain_whole(last - 1, corner)
+    chain_split(last - 1, middle, True)
+    chain_whole(last - 1, middle, True)
+    chain_whole(last, corner)
+    chain_split(last, middle, True)
+    chain_whole(last, middle, True)
+    chain_split(last - 2, middle, True)
+    chain_whole(last - 2, middle, True)
+    chain_whole(last - 2, corner)
     for q in range(z_pieces):
         await_ends(pieces + q)
         y_out[0, q] = (pair_sum(0, 1, q) + ends(pieces + q)).astype(bf16)
-        launch([across_copy(0, q)])
+        across_copy(0, q).start()
     for p in list(range(z_pieces, pieces)) + list(range(z_pieces)):
         await_ends(p)
         total = pair_sum(0, 0, p) + ends(p)
         across_copy(0, p).wait_recv()
         out_ref[:, pl.ds(p * span, span)] = (total + y_in[0, p].astype(f32)).astype(bf16)
-    for step in range(1, depth):
-        for j in range(pieces + z_pieces):
-            note_hop(step, j)
-    for copies, cond in pending:
-        def finish(copies=copies):
-            for copy in copies:
-                copy.wait_send()
-        if cond is None:
-            finish()
-        else:
-            pl.when(cond)(finish)
+    finish_gather()
+    for step in range(depth):
+        for k in range(2):
+            remote(
+                part.at[step, k, 1 - c], a_in.at[step, k], sa.at[step, k], ra.at[step, k, 0], sibling
+            ).wait_send()
+        some = pl.ds(0, pieces) if step == 0 else pl.ds(z_pieces, pieces - z_pieces)
+        remote(
+            y_out.at[step, some], y_in.at[step, some], sy.at[step], ry.at[step, 0], across
+        ).wait_send()
+        if step > 0:
+            remote(
+                c_out.at[step], c_in.at[0, 0], sc.at[step], rc.at[0, 0, 0], sibling
+            ).wait_send()
 
 
 def fused_layer(tokens, ids, gates, w_gate, w_up, w_down, expert_total, depth):
@@ -450,7 +490,6 @@
     anywhere = pl.BlockSpec(memory_space=pl.ANY)
     inside = pl.BlockSpec(memory_space=pltpu.VMEM)
     span = width // pieces
-    sends = depth * (6 * chunks + 2)
     lots = pieces + z_pieces
     return pl.pallas_call(
         functools.partial(fused_kernel, depth),
@@ -459,7 +498,7 @@
         out_specs=pl.BlockSpec(memory_space=pltpu.VMEM),
         scratch_shapes=[
             pltpu.VMEM((depth, 4, local, width), bf16),
-            pltpu.VMEM((depth, 4, expert_total, 128), f32),
+            pltpu.VMEM((depth, 2, 2, expert_total, 128), f32),
             pltpu.VMEM((width, inner), bf16),
             pltpu.VMEM((width, inner), bf16),
             pltpu.VMEM((inner, width), bf16),
@@ -471,10 +510,10 @@
             pltpu.VMEM((depth, lots, local, span), bf16),
             pltpu.VMEM((2, depth, lots, local, span), bf16),
             dma((3,)), dma((1,)),
-            dma((sends,)), dma((depth, 4, chunks)), dma((5 * depth,)), dma((depth, 4)),
-            dma((depth, 2, 3)), dma((depth, 2, 3)),
-            dma((depth, pieces)), dma((depth, pieces)),
-            dma((depth, lots)), dma((2, depth, lots)),
+            dma((10 * depth,)), dma((depth, 4, chunks)), dma((2 * depth + 4,)), dma((depth + 2,)),
+            dma((depth, 2)), dma((depth, 2, 2)),
+            dma((depth,)), dma((depth, pieces)),
+            dma((depth,)), dma((2, depth, lots)),
         ],
         compiler_params=pltpu.CompilerParams(
             collective_id=0, has_side_effects=True, vmem_limit_bytes=60 * 2**20
@@ -487,7 +526,7 @@
     weights = 6 * model_width * inner
     return (
         device_count % 4 == 0
-        and device_count >= 8
+        and device_count // 4 == 4
         and local_tokens in (64, 128)
         and local_tokens % (16 * chunks) == 0
         and model_width % (pieces * 128) == 0

time: 68.5 us -> 63 us (0.920)
  Pallas kernels: 66.6 us -> 61.1 us
    pallas_call x1, Pallas kernels: 66.6 us -> 61.1 us  [fused_layer(): pl.pallas_call(functools.partial(fused_kernel, depth), out_shape=jax.Shap...]
where the time goes in v2:
time: 63 us; the launch traced here: 62.8 us
  Pallas kernels  61.1 us (97%)
  local copies, waits for them, and re-layouts  1.67 us (3%)
    pallas_call x1, Pallas kernels, fused_layer(): pl.pallas_call(functools.partial(fused_kernel, depth), out_shape=jax.Shap...  61.1 us
    unnamed x1, local copies, waits for them, and re-layouts  1.67 us

profile of v2, /device:TPU:0, one launch (start us, length us, event | category | flops | bytes accessed | tf_op | source)
XLA Modules:
  0.0 62.8 jit_solution(3054113173899106688)
XLA Ops:
  0.0 61.1 %shard_map.64 = bf16[64,2048]{1,0:T(8,128)(2,1)} custom-call(bf16[64,2048]{1,0:T(8,128)(2,1)} %x_hbm.1, s32[8,64]{1,0:T(8,128)} %bitcast.2, f32[8,64]{1,0:T(8,128)} %bitcast.3, bf16[1,2048,768]{2,1,0:T(8,128)(2,1)} %wg_hbm.1, bf16[1,2048,768]{2,1,0:T(8,128)(2,1)} %wu_hbm.1, bf16[1,768,2048]{2,1,0:T(8,128)(2,1)} %wd_hbm.1), custom_call_target="tpu_custom_call" | custom-call | tf_op jit(solution)/shard_map/pallas_call | solution.py:494
  61.1 1.7 %copy.8 = bf16[64,2048]{1,0:T(8,128)(2,1)} copy(bf16[64,2048]{1,0:T(8,128)(2,1)} %shard_map.64) | data formatting | bytes 524288

commit v3 on v2

--- a/solution.py
+++ b/solution.py
@@ -7,7 +7,7 @@
 from jax.sharding import PartitionSpec as P
 
 row_block = 256
-pieces = 4
+pieces = 8
 chunks = 4
 late_chunks = 1
 z_pieces = 0
@@ -446,11 +446,11 @@
     drain(len(work))
     send_across(last)
     send_across(last - 2)
-    send_across(0)
     chain_split(last, corner)
     chain_whole(last - 1, corner)
     chain_split(last - 1, middle, True)
     chain_whole(last - 1, middle, True)
+    send_across(0)
     chain_whole(last, corner)
     chain_split(last, middle, True)
     chain_whole(last, middle, True)

time: 63 us -> 62.6 us (level)
  no operation moved by 1% of the time
where the time goes in v3:
time: 62.6 us; the launch traced here: 62.4 us
  Pallas kernels  60.8 us (97%)
  local copies, waits for them, and re-layouts  1.67 us (3%)
    pallas_call x1, Pallas kernels, fused_layer(): pl.pallas_call(functools.partial(fused_kernel, depth), out_shape=jax.Shap...  60.8 us
    unnamed x1, local copies, waits for them, and re-layouts  1.67 us

profile of v3, /device:TPU:0, one launch (start us, length us, event | category | flops | bytes accessed | tf_op | source)
XLA Modules:
  0.0 62.4 jit_solution(9538409739998008233)
XLA Ops:
  0.0 60.8 %shard_map.64 = bf16[64,2048]{1,0:T(8,128)(2,1)} custom-call(bf16[64,2048]{1,0:T(8,128)(2,1)} %x_hbm.1, s32[8,64]{1,0:T(8,128)} %bitcast.2, f32[8,64]{1,0:T(8,128)} %bitcast.3, bf16[1,2048,768]{2,1,0:T(8,128)(2,1)} %wg_hbm.1, bf16[1,2048,768]{2,1,0:T(8,128)(2,1)} %wu_hbm.1, bf16[1,768,2048]{2,1,0:T(8,128)(2,1)} %wd_hbm.1), custom_call_target="tpu_custom_call" | custom-call | tf_op jit(solution)/shard_map/pallas_call | solution.py:494
  60.8 1.7 %copy.8 = bf16[64,2048]{1,0:T(8,128)(2,1)} copy(bf16[64,2048]{1,0:T(8,128)(2,1)} %shard_map.64) | data formatting | bytes 524288
